TPU v7x, 512 devices: a whole 4x4x16 slice. The times are simulated.
512 devices in a mesh: dp: 32 (over z, core), seq: 16 (over y, x).
Axes of the slice: x: 4, y: 4, z: 16, core: 2. Of those that a mesh axis runs over, the one named last changes fastest.
Arguments:
- features: bfloat16 [32, 3072, 1024], P('dp', 'seq'), may hold values from -18 to 18
- qkv_weight: bfloat16 [1024, 3072], P('dp'), may hold values from -1 to 1
- cotangent: bfloat16 [32, 3072, 1024], P('dp', 'seq'), may hold values from -6 to 6
- node_order: int32 [32, 3072], P('dp'), may hold values from 0 to 3071, as said below
- blocks: int32 [32, 48, 8], P('dp'), may hold values from 0 to 47, as said below
- counts: int32 [32, 48], P('dp'), may hold values from 1 to 8, as said below
Outputs:
- attended: bfloat16 [32, 3072, 1024], P('dp', 'seq')
- grad_features: bfloat16 [32, 3072, 1024], P('dp', 'seq')
- grad_weight: float32 [1024, 3072], P('dp', 'seq')
Inputs may be any that keep to these rules, and one draw needn't show every extreme that they name: Every row of node_order lists each node of the subgraph once. blocks[g, c, 0] is c, and the 8 entries of a row are distinct clusters; slots at or beyond counts[g, c] are unused. `counts`: every subgraph has a cluster with all 8 slots live.
All inputs are finite; a program needn't handle non-finite values.
Results may differ from a plain program's by a relative error of at most 0.03.
Values may be sent and summed in bfloat16 or wider, within the bound.
No kernel may reach another device: no remote copies, remote signals or barrier semaphores. Data moves between devices by JAX's collectives and lax.ppermute only.
A program may use at most 128 MiB of HBM per device.

v0:
```python
import math
import jax
import jax.numpy as jnp
from jax import lax
from jax.sharding import PartitionSpec as P

HEADS = 16
HD = 64


def attend(query, key_in, value, grad_out, blocks, counts):
    cluster_count, slot_count = blocks.shape
    node_count, head_width = query.shape
    block_rows = node_count // cluster_count
    in_group = math.gcd(cluster_count, 8)
    runs_total = cluster_count // in_group
    score_scale = 1.0 / math.sqrt(head_width)
    key_blocks = key_in.reshape(cluster_count, block_rows, head_width)
    value_blocks = value.reshape(cluster_count, block_rows, head_width)
    inputs_all = (
        query.reshape(runs_total, in_group, block_rows, head_width),
        grad_out.reshape(runs_total, in_group, block_rows, head_width),
        blocks.reshape(runs_total, in_group, slot_count),
        counts.reshape(runs_total, in_group),
    )

    def group_step(totals, inputs_now):
        grad_key, grad_value = totals
        query_block, grad_block, block_ids, live_count = inputs_now
        key_rows = key_blocks[block_ids].reshape(in_group, slot_count * block_rows, head_width)
        value_rows = value_blocks[block_ids].reshape(in_group, slot_count * block_rows, head_width)
        is_live = jnp.repeat(
            jnp.arange(slot_count)[None, :] < live_count[:, None], block_rows, axis=1
        )[:, None, :]
        scores = (
            jnp.einsum("cqe,cke->cqk", query_block, key_rows, preferred_element_type=jnp.float32)
            * score_scale
        )
        scores = jnp.where(is_live, scores, -1e30)
        row_max = jnp.max(scores, axis=-1, keepdims=True)
        raw_weights = jnp.where(is_live, jnp.exp(scores - row_max), 0.0)
        attn_weights = raw_weights / jnp.sum(raw_weights, axis=-1, keepdims=True)
        attn_low = attn_weights.astype(jnp.bfloat16)
        output_blk = jnp.einsum(
            "cqk,cke->cqe", attn_low, value_rows, preferred_element_type=jnp.float32
        ).astype(jnp.bfloat16)
        grad_weights = jnp.einsum(
            "cqe,cke->cqk", grad_block, value_rows, preferred_element_type=jnp.float32
        )
        row_dot = jnp.sum(attn_weights * grad_weights, axis=-1, keepdims=True)
        grad_scores = (attn_weights * (grad_weights - row_dot) * score_scale).astype(jnp.bfloat16)
        grad_query = jnp.einsum(
            "cqk,cke->cqe", grad_scores, key_rows, preferred_element_type=jnp.float32
        ).astype(jnp.bfloat16)
        key_terms = jnp.einsum(
            "cqk,cqe->cke", grad_scores, query_block, preferred_element_type=jnp.float32
        )
        value_terms = jnp.einsum(
            "cqk,cqe->cke", attn_low, grad_block, preferred_element_type=jnp.float32
        )
        grad_key = grad_key.at[block_ids].add(
            key_terms.reshape(in_group, slot_count, block_rows, head_width)
        )
        grad_value = grad_value.at[block_ids].add(
            value_terms.reshape(in_group, slot_count, block_rows, head_width)
        )
        return ((grad_key, grad_value), (output_blk, grad_query))

    empty_sum = jnp.zeros((cluster_count, block_rows, head_width), jnp.float32)
    (grad_key, grad_value), (output_all, grad_query) = lax.scan(
        group_step, (empty_sum, empty_sum), inputs_all
    )
    return (
        output_all.reshape(node_count, head_width),
        grad_query.reshape(node_count, head_width),
        grad_key.reshape(node_count, head_width).astype(jnp.bfloat16),
        grad_value.reshape(node_count, head_width).astype(jnp.bfloat16),
    )


def per_device(features, qkv_weight, cotangent, node_order, blocks, counts):
    local_rows = features.shape[1]
    model_width = features.shape[2]
    heads_local = HEADS // lax.axis_size("seq")
    three_width = 3 * HD
    node_feats = features[0]
    cot_heads = cotangent[0].reshape(local_rows, HEADS, HD)
    weights_all = lax.all_gather(qkv_weight, "dp", axis=0, tiled=True)
    node_all = lax.all_gather(node_feats, "seq", axis=0, tiled=True)
    node_count = node_all.shape[0]
    projected = jnp.dot(node_feats, weights_all, preferred_element_type=jnp.float32).astype(
        jnp.bfloat16
    )
    projected = projected.reshape(local_rows, HEADS, three_width)
    head_qkv, head_cot = (
        lax.all_to_all(projected, "seq", split_axis=1, concat_axis=0, tiled=True),
        lax.all_to_all(cot_heads, "seq", split_axis=1, concat_axis=0, tiled=True),
    )
    graph_order = node_order[0]
    inverse = (
        jnp.zeros((node_count,), jnp.int32)
        .at[graph_order]
        .set(jnp.arange(node_count, dtype=jnp.int32))
    )
    sorted_qkv = head_qkv[graph_order]
    sorted_cot = head_cot[graph_order]
    output_all, grad_query, grad_key, grad_value = jax.vmap(
        attend, in_axes=(1, 1, 1, 1, None, None), out_axes=1
    )(
        sorted_qkv[:, :, :HD],
        sorted_qkv[:, :, HD : 2 * HD],
        sorted_qkv[:, :, 2 * HD :],
        sorted_cot,
        blocks[0],
        counts[0],
    )
    grad_heads = jnp.concatenate([grad_query, grad_key, grad_value], axis=-1)[inverse]
    output_nodes = output_all[inverse]
    output_back, grad_back = (
        lax.all_to_all(output_nodes, "seq", split_axis=0, concat_axis=1, tiled=True),
        lax.all_to_all(grad_heads, "seq", split_axis=0, concat_axis=1, tiled=True),
    )
    attended = output_back.reshape(1, local_rows, model_width)
    grad_local = grad_back.reshape(local_rows, 3 * model_width)
    grad_feats = lax.dot_general(
        grad_local, weights_all, (((1,), (1,)), ((), ())), preferred_element_type=jnp.float32
    )
    grad_features = grad_feats.astype(jnp.bfloat16).reshape(1, local_rows, model_width)
    head_grads = grad_heads.reshape(node_count, heads_local * three_width)
    grad_weight = lax.psum_scatter(
        lax.dot_general(
            node_all, head_grads, (((0,), (0,)), ((), ())), preferred_element_type=jnp.float32
        ).astype(jnp.bfloat16),
        "dp",
        scatter_dimension=0,
        tiled=True,
    ).astype(jnp.float32)
    return (attended, grad_features, grad_weight)


def solution(mesh):
    return jax.shard_map(
        per_device,
        mesh=mesh,
        in_specs=(
            P("dp", "seq", None),
            P("dp", None),
            P("dp", "seq", None),
            P("dp", None),
            P("dp", None, None),
            P("dp", None),
        ),
        out_specs=(P("dp", "seq", None), P("dp", "seq", None), P("dp", "seq")),
        check_vma=False,
    )
```

profile of v0, /device:TPU:8, one launch (start us, length us, event | category | flops | bytes accessed | tf_op | source)
XLA Modules:
  0.0 628.1 jit_solution(6024842970168261089)
XLA Ops:
  9.9 9.2 %all-to-all-start.1 = ((bf16[192,16,64]{0,2,1:T(8,128)(2,1)}), bf16[192,16,64]{0,2,1:T(8,128)(2,1)S(1)}, u32[]{:S(2)}, u32[]{:S(2)}) async-start(bf16[192,16,64]{0,2,1:T(8,128)(2,1)} %bitcast.27), calls=%async_computation.1 | async-start | bytes 1048576 | tf_op jit(solution)/shard_map/all_to_all | solution.py:97
  21.2 70.2 %all-gather.4.cloned.1.call-done = bf16[1024,3072]{1,0:T(8,128)(2,1)} async-done(((bf16[32,3072]{1,0:T(8,128)(2,1)}), bf16[1024,3072]{1,0:T(8,128)(2,1)}) %all-gather.4.cloned.1.call-update) | async-done | bytes 6291472 | tf_op jit(solution)/shard_map/all_gather | solution.py:88
  101.5 7.4 %all-to-all-start = ((bf16[192,16,192]{2,0,1:T(8,128)(2,1)}), bf16[192,16,192]{2,0,1:T(8,128)(2,1)S(1)}, u32[]{:S(2)}, u32[]{:S(2)}) async-start(bf16[192,16,192]{2,0,1:T(8,128)(2,1)} %copy.93), calls=%async_computation | async-start | bytes 3145728 | tf_op jit(solution)/shard_map/all_to_all | solution.py:96
  108.9 12.0 %scatter_custom_fusion.2 = s32[3072]{0:T(1024)S(1)} fusion(s32[3072]{0:T(1024)S(1)} %bitcast.182, s32[3072]{0:T(1024)S(1)} %iota.7, s32[]{:T(128)} %copy.139), kind=kCustom, calls=%fused_computation.71 | custom fusion | bytes 12292 | tf_op jit(solution)/shard_map/scatter | solution.py:103
  121.3 11.4 %gather_fusion.3 = bf16[3072,64]{1,0:T(8,128)(2,1)} fusion(bf16[3072,64]{1,0:T(8,128)(2,1)S(1)} %bitcast.161, s32[3072]{0:T(1024)S(1)} %broadcast_clamp_fusion), kind=kCustom, calls=%fused_computation.3 | custom fusion | bytes 798720 | tf_op jit(solution)/shard_map/gather | solution.py:106
  137.2 11.1 %gather_fusion.2 = bf16[3072,192]{1,0:T(8,128)(2,1)S(1)} fusion(bf16[3072,192]{1,0:T(8,128)(2,1)S(1)} %bitcast.152, s32[3072]{0:T(1024)S(1)} %broadcast_clamp_fusion), kind=kCustom, calls=%fused_computation.2 | custom fusion | bytes 2371584 | tf_op jit(solution)/shard_map/gather | solution.py:105
  150.4 286.3 %while.16 = (s32[]{:T(128)}, f32[1,48,64,64]{3,2,1,0:T(8,128)S(1)}, f32[1,48,64,64]{3,2,1,0:T(8,128)S(1)}, bf16[6,1,8,64,64]{4,3,2,1,0:T(8,128)(2,1)}, bf16[6,1,...) while((s32[]{:T(128)}, f32[1,48,64,64]{3,2,1,0:T(8,128)S(1)}, ...), condition=%wide.region_6.7_spmd, body=%wide.region_0.6_spmd.sunk | while | flops 209000192 | bytes 36499064 | solution.py:70
  173.6 7.0 %scatter_fusion.1 = f32[48,64,64]{2,1,0:T(8,128)S(1)} fusion(f32[48,64,64]{2,1,0:T(8,128)S(1)} %bitcast.155, s32[64]{0:T(128)S(1)} %reshape.343, f32[64,64,64]{2,1,0:T(8,128)} %bitcast.163), kind=kCustom, calls=%fused_computation.7.clone.1 | custom fusion | flops 262144 | bytes 3145984 | tf_op jit(solution)/shard_map/vmap()/while/body/eval_jaxpr/scatter-add | solution.py:64
  180.6 7.0 %fusion.110 = f32[8,512,64]{2,1,0:T(8,128)} fusion(f32[8,64,512]{2,1,0:T(8,128)} %fusion.106, bf16[6,1,8,64,64]{4,3,2,1,0:T(8,128)(2,1)} %get-tuple-element.266, s32[]{:T(128)} %get-tuple-element.247, f32[8,64,512]{2,1,0:T(8,128)} %get-tuple-element.233, f32[8,64]{1,0:T(8,128)S(1)} %get-tuple-element.234), kind=kOutput, calls=%fused_computation.26.clone.1 | convolution fusion | flops 35390464 | bytes 5382656 | tf_op jit(solution)/shard_map/vmap()/while/body/eval_jaxpr/reshape | solution.py:62
  187.7 7.0 %scatter_fusion = f32[48,64,64]{2,1,0:T(8,128)S(1)} fusion(f32[48,64,64]{2,1,0:T(8,128)S(1)} %bitcast.153, s32[64]{0:T(128)S(1)} %reshape.343, f32[64,64,64]{2,1,0:T(8,128)} %bitcast.162), kind=kCustom, calls=%fused_computation.6.clone.1 | custom fusion | flops 262144 | bytes 3145984 | tf_op jit(solution)/shard_map/vmap()/while/body/eval_jaxpr/scatter-add | solution.py:61
  221.3 7.0 %scatter_fusion.1 = f32[48,64,64]{2,1,0:T(8,128)S(1)} fusion(f32[48,64,64]{2,1,0:T(8,128)S(1)} %bitcast.155, s32[64]{0:T(128)S(1)} %reshape.343, f32[64,64,64]{2,1,0:T(8,128)} %bitcast.163), kind=kCustom, calls=%fused_computation.7.clone.1 | custom fusion | flops 262144 | bytes 3145984 | tf_op jit(solution)/shard_map/vmap()/while/body/eval_jaxpr/scatter-add | solution.py:64
  228.3 7.0 %fusion.110 = f32[8,512,64]{2,1,0:T(8,128)} fusion(f32[8,64,512]{2,1,0:T(8,128)} %fusion.106, bf16[6,1,8,64,64]{4,3,2,1,0:T(8,128)(2,1)} %get-tuple-element.266, s32[]{:T(128)} %get-tuple-element.247, f32[8,64,512]{2,1,0:T(8,128)} %get-tuple-element.233, f32[8,64]{1,0:T(8,128)S(1)} %get-tuple-element.234), kind=kOutput, calls=%fused_computation.26.clone.1 | convolution fusion | flops 35390464 | bytes 5382656 | tf_op jit(solution)/shard_map/vmap()/while/body/eval_jaxpr/reshape | solution.py:62
  235.4 7.0 %scatter_fusion = f32[48,64,64]{2,1,0:T(8,128)S(1)} fusion(f32[48,64,64]{2,1,0:T(8,128)S(1)} %bitcast.153, s32[64]{0:T(128)S(1)} %reshape.343, f32[64,64,64]{2,1,0:T(8,128)} %bitcast.162), kind=kCustom, calls=%fused_computation.6.clone.1 | custom fusion | flops 262144 | bytes 3145984 | tf_op jit(solution)/shard_map/vmap()/while/body/eval_jaxpr/scatter-add | solution.py:61
  269.0 7.0 %scatter_fusion.1 = f32[48,64,64]{2,1,0:T(8,128)S(1)} fusion(f32[48,64,64]{2,1,0:T(8,128)S(1)} %bitcast.155, s32[64]{0:T(128)S(1)} %reshape.343, f32[64,64,64]{2,1,0:T(8,128)} %bitcast.163), kind=kCustom, calls=%fused_computation.7.clone.1 | custom fusion | flops 262144 | bytes 3145984 | tf_op jit(solution)/shard_map/vmap()/while/body/eval_jaxpr/scatter-add | solution.py:64
  276.0 7.0 %fusion.110 = f32[8,512,64]{2,1,0:T(8,128)} fusion(f32[8,64,512]{2,1,0:T(8,128)} %fusion.106, bf16[6,1,8,64,64]{4,3,2,1,0:T(8,128)(2,1)} %get-tuple-element.266, s32[]{:T(128)} %get-tuple-element.247, f32[8,64,512]{2,1,0:T(8,128)} %get-tuple-element.233, f32[8,64]{1,0:T(8,128)S(1)} %get-tuple-element.234), kind=kOutput, calls=%fused_computation.26.clone.1 | convolution fusion | flops 35390464 | bytes 5382656 | tf_op jit(solution)/shard_map/vmap()/while/body/eval_jaxpr/reshape | solution.py:62
  283.1 7.0 %scatter_fusion = f32[48,64,64]{2,1,0:T(8,128)S(1)} fusion(f32[48,64,64]{2,1,0:T(8,128)S(1)} %bitcast.153, s32[64]{0:T(128)S(1)} %reshape.343, f32[64,64,64]{2,1,0:T(8,128)} %bitcast.162), kind=kCustom, calls=%fused_computation.6.clone.1 | custom fusion | flops 262144 | bytes 3145984 | tf_op jit(solution)/shard_map/vmap()/while/body/eval_jaxpr/scatter-add | solution.py:61
  316.7 7.0 %scatter_fusion.1 = f32[48,64,64]{2,1,0:T(8,128)S(1)} fusion(f32[48,64,64]{2,1,0:T(8,128)S(1)} %bitcast.155, s32[64]{0:T(128)S(1)} %reshape.343, f32[64,64,64]{2,1,0:T(8,128)} %bitcast.163), kind=kCustom, calls=%fused_computation.7.clone.1 | custom fusion | flops 262144 | bytes 3145984 | tf_op jit(solution)/shard_map/vmap()/while/body/eval_jaxpr/scatter-add | solution.py:64
  323.8 7.0 %fusion.110 = f32[8,512,64]{2,1,0:T(8,128)} fusion(f32[8,64,512]{2,1,0:T(8,128)} %fusion.106, bf16[6,1,8,64,64]{4,3,2,1,0:T(8,128)(2,1)} %get-tuple-element.266, s32[]{:T(128)} %get-tuple-element.247, f32[8,64,512]{2,1,0:T(8,128)} %get-tuple-element.233, f32[8,64]{1,0:T(8,128)S(1)} %get-tuple-element.234), kind=kOutput, calls=%fused_computation.26.clone.1 | convolution fusion | flops 35390464 | bytes 5382656 | tf_op jit(solution)/shard_map/vmap()/while/body/eval_jaxpr/reshape | solution.py:62
  330.8 7.0 %scatter_fusion = f32[48,64,64]{2,1,0:T(8,128)S(1)} fusion(f32[48,64,64]{2,1,0:T(8,128)S(1)} %bitcast.153, s32[64]{0:T(128)S(1)} %reshape.343, f32[64,64,64]{2,1,0:T(8,128)} %bitcast.162), kind=kCustom, calls=%fused_computation.6.clone.1 | custom fusion | flops 262144 | bytes 3145984 | tf_op jit(solution)/shard_map/vmap()/while/body/eval_jaxpr/scatter-add | solution.py:61
  354.2 6.0 fusion.113
  364.4 7.0 %scatter_fusion.1 = f32[48,64,64]{2,1,0:T(8,128)S(1)} fusion(f32[48,64,64]{2,1,0:T(8,128)S(1)} %bitcast.155, s32[64]{0:T(128)S(1)} %reshape.343, f32[64,64,64]{2,1,0:T(8,128)} %bitcast.163), kind=kCustom, calls=%fused_computation.7.clone.1 | custom fusion | flops 262144 | bytes 3145984 | tf_op jit(solution)/shard_map/vmap()/while/body/eval_jaxpr/scatter-add | solution.py:64
  371.5 7.0 %fusion.110 = f32[8,512,64]{2,1,0:T(8,128)} fusion(f32[8,64,512]{2,1,0:T(8,128)} %fusion.106, bf16[6,1,8,64,64]{4,3,2,1,0:T(8,128)(2,1)} %get-tuple-element.266, s32[]{:T(128)} %get-tuple-element.247, f32[8,64,512]{2,1,0:T(8,128)} %get-tuple-element.233, f32[8,64]{1,0:T(8,128)S(1)} %get-tuple-element.234), kind=kOutput, calls=%fused_computation.26.clone.1 | convolution fusion | flops 35390464 | bytes 5382656 | tf_op jit(solution)/shard_map/vmap()/while/body/eval_jaxpr/reshape | solution.py:62
  378.5 7.0 %scatter_fusion = f32[48,64,64]{2,1,0:T(8,128)S(1)} fusion(f32[48,64,64]{2,1,0:T(8,128)S(1)} %bitcast.153, s32[64]{0:T(128)S(1)} %reshape.343, f32[64,64,64]{2,1,0:T(8,128)} %bitcast.162), kind=kCustom, calls=%fused_computation.6.clone.1 | custom fusion | flops 262144 | bytes 3145984 | tf_op jit(solution)/shard_map/vmap()/while/body/eval_jaxpr/scatter-add | solution.py:61
  412.2 7.0 %scatter_fusion.1 = f32[48,64,64]{2,1,0:T(8,128)S(1)} fusion(f32[48,64,64]{2,1,0:T(8,128)S(1)} %bitcast.155, s32[64]{0:T(128)S(1)} %reshape.343, f32[64,64,64]{2,1,0:T(8,128)} %bitcast.163), kind=kCustom, calls=%fused_computation.7.clone.1 | custom fusion | flops 262144 | bytes 3145984 | tf_op jit(solution)/shard_map/vmap()/while/body/eval_jaxpr/scatter-add | solution.py:64
  419.2 7.0 %fusion.110 = f32[8,512,64]{2,1,0:T(8,128)} fusion(f32[8,64,512]{2,1,0:T(8,128)} %fusion.106, bf16[6,1,8,64,64]{4,3,2,1,0:T(8,128)(2,1)} %get-tuple-element.266, s32[]{:T(128)} %get-tuple-element.247, f32[8,64,512]{2,1,0:T(8,128)} %get-tuple-element.233, f32[8,64]{1,0:T(8,128)S(1)} %get-tuple-element.234), kind=kOutput, calls=%fused_computation.26.clone.1 | convolution fusion | flops 35390464 | bytes 5382656 | tf_op jit(solution)/shard_map/vmap()/while/body/eval_jaxpr/reshape | solution.py:62
  426.2 7.0 %scatter_fusion = f32[48,64,64]{2,1,0:T(8,128)S(1)} fusion(f32[48,64,64]{2,1,0:T(8,128)S(1)} %bitcast.153, s32[64]{0:T(128)S(1)} %reshape.343, f32[64,64,64]{2,1,0:T(8,128)} %bitcast.162), kind=kCustom, calls=%fused_computation.6.clone.1 | custom fusion | flops 262144 | bytes 3145984 | tf_op jit(solution)/shard_map/vmap()/while/body/eval_jaxpr/scatter-add | solution.py:61
  438.9 9.2 %gather_fusion.4 = bf16[3072,64]{1,0:T(8,128)(2,1)S(1)} fusion(bf16[3072,64]{1,0:T(8,128)(2,1)S(1)} %bitcast.164, s32[3072]{0:T(1024)S(1)} %fusion.52), kind=kCustom, calls=%fused_computation.4 | custom fusion | bytes 798720 | tf_op jit(solution)/shard_map/gather | solution.py:118
  459.1 11.1 %gather_fusion.5 = bf16[3072,192]{1,0:T(8,128)(2,1)S(1)} fusion(bf16[3072,192]{1,0:T(8,128)(2,1)S(1)} %maximum_bitcast_fusion, s32[3072]{0:T(1024)S(1)} %fusion.52), kind=kCustom, calls=%fused_computation.5 | custom fusion | bytes 2371584 | tf_op jit(solution)/shard_map/gather | solution.py:117
  474.5 7.3 %all-to-all-start.3 = ((bf16[16,2,18432]{2,1,0:T(2,128)(2,1)}), bf16[16,2,18432]{2,1,0:T(2,128)(2,1)}, u32[]{:S(2)}, u32[]{:S(2)}) async-start(bf16[16,2,18432]{2,1,0:T(2,128)(2,1)} %reshape.324), calls=%async_computation.3 | async-start | bytes 2359296 | tf_op jit(solution)/shard_map/all_to_all | solution.py:121
  491.1 101.6 %reduce-scatter.4.cloned.1.call-done = bf16[32,192]{1,0:T(8,128)(2,1)} async-done(((bf16[1024,192]{1,0:T(8,128)(2,1)}), bf16[32,192]{1,0:T(8,128)(2,1)}) %reduce-scatter.4.cloned.1.call-update) | async-done | bytes 12304
  594.2 8.4 %reshape.325 = bf16[3072,1,192]{2,1,0:T(2,128)(2,1)S(1)} reshape(bf16[16,2,18432]{2,1,0:T(2,128)(2,1)} %all-to-all-done.3) | data formatting | bytes 2359296
  602.6 6.2 copy.102
  (164 shorter events, 216.7 us)
Async XLA Ops:
  7.2 84.3 %copy-start.3 = (bf16[1,192,1024]{2,1,0:T(8,128)(2,1)S(1)}, bf16[1,192,1024]{2,1,0:T(8,128)(2,1)}, u32[]{:S(2)}) copy-start(bf16[1,192,1024]{2,1,0:T(8,128)(2,1)} %param.8) | copy-start | bytes 1179652
  7.2 12.7 %copy-start.5 = (s32[1,48,8]{1,2,0:T(8,128)S(1)}, s32[1,48,8]{1,2,0:T(8,128)}, u32[]{:S(2)}) copy-start(s32[1,48,8]{1,2,0:T(8,128)} %param.12) | copy-start | bytes 4612
  7.2 13.3 %copy-start.6 = (s32[1,48]{1,0:T(1,128)S(1)}, s32[1,48]{1,0:T(1,128)}, u32[]{:S(2)}) copy-start(s32[1,48]{1,0:T(1,128)} %param.13) | copy-start | bytes 580
  7.2 84.3 %all-gather.4.cloned.1.call-start = ((), (), s32[]{:S(2)}) async-start(), calls=%async_computation.5 | async-start | bytes 6488064 | tf_op jit(solution)/shard_map/all_gather | solution.py:88
  9.9 91.6 %all-to-all-start.1 = ((bf16[192,16,64]{0,2,1:T(8,128)(2,1)}), bf16[192,16,64]{0,2,1:T(8,128)(2,1)S(1)}, u32[]{:S(2)}, u32[]{:S(2)}) async-start(bf16[192,16,64]{0,2,1:T(8,128)(2,1)} %bitcast.27), calls=%async_computation.1 | async-start | bytes 1048576 | tf_op jit(solution)/shard_map/all_to_all | solution.py:97
  19.1 462.7 %all-gather.6.cloned.1.call-start = ((), (), s32[]{:S(2)}) async-start(), calls=%async_computation.6 | async-start | bytes 6684672 | tf_op jit(solution)/shard_map/all_gather | solution.py:89
  101.5 7.4 %copy-start.4 = (s32[1,3072]{1,0:T(1,128)S(1)}, s32[1,3072]{1,0:T(1,128)}, u32[]{:S(2)}) copy-start(s32[1,3072]{1,0:T(1,128)} %param.11) | copy-start | bytes 36868
  101.5 35.7 %all-to-all-start = ((bf16[192,16,192]{2,0,1:T(8,128)(2,1)}), bf16[192,16,192]{2,0,1:T(8,128)(2,1)S(1)}, u32[]{:S(2)}, u32[]{:S(2)}) async-start(bf16[192,16,192]{2,0,1:T(8,128)(2,1)} %copy.93), calls=%async_computation | async-start | bytes 3145728 | tf_op jit(solution)/shard_map/all_to_all | solution.py:96
  155.4 1.0 copy-start
  203.2 1.0 copy-start
  250.9 1.0 copy-start
  298.6 1.0 copy-start
  346.3 1.0 copy-start
  394.0 1.0 copy-start
  437.8 1.1 copy-start.1
  448.6 8.6 %copy-start.2 = (bf16[1,48,64,64]{3,2,1,0:T(8,128)(2,1)S(1)}, bf16[1,48,64,64]{3,2,1,0:T(8,128)(2,1)}, u32[]{:S(2)}) copy-start(bf16[1,48,64,64]{3,2,1,0:T(8,128)(2,1)} %convert_element_type.62) | copy-start | bytes 1179652
  451.4 23.1 %all-to-all-start.2 = ((bf16[16,2,6144]{2,1,0:T(2,128)(2,1)}), bf16[16,2,6144]{2,1,0:T(2,128)(2,1)S(1)}, u32[]{:S(2)}, u32[]{:S(2)}) async-start(bf16[16,2,6144]{2,1,0:T(2,128)(2,1)} %reshape.322), calls=%async_computation.2 | async-start | bytes 786432 | tf_op jit(solution)/shard_map/all_to_all | solution.py:120
  474.5 119.7 %all-to-all-start.3 = ((bf16[16,2,18432]{2,1,0:T(2,128)(2,1)}), bf16[16,2,18432]{2,1,0:T(2,128)(2,1)}, u32[]{:S(2)}, u32[]{:S(2)}) async-start(bf16[16,2,18432]{2,1,0:T(2,128)(2,1)} %reshape.324), calls=%async_computation.3 | async-start | bytes 2359296 | tf_op jit(solution)/shard_map/all_to_all | solution.py:121
  481.7 110.9 %reduce-scatter.4.cloned.1.call-start = ((), (), s32[]{:S(2)}) async-start(), calls=%async_computation.7 | async-start | bytes 540672
Sparse Core Ops, SparseCore 0:
  10.2 81.2 all-gather.3
  94.5 83.8 all-gather.5
  487.2 105.4 reduce-scatter.3
where the time goes:
time: 633 us; the launch traced here: 628 us
  waiting for transfers between devices  178 us (28%)
  matrix products  168 us (27%)
  local copies, waits for them, and re-layouts  140 us (22%)
  other arithmetic  99 us (16%)
  starting transfers between devices  29.8 us (5%)
  between operations  14 us (2%)
    unnamed x4, waiting for transfers between devices  103 us
    all_gather x1, waiting for transfers between devices, per_device(): weights_all = lax.all_gather(qkv_weight, 'dp', axis=0, tiled=True)  70.2 us
    reshape x6, matrix products, group_step(): key_terms.reshape(in_group, slot_count, block_rows, head_width)  42.2 us
    scatter-add x6, other arithmetic, group_step(): grad_value.at[block_ids]  42 us
    scatter-add x6, other arithmetic, group_step(): grad_key.at[block_ids]  42 us
    dot_general x6, matrix products, group_step(): jnp.einsum('cqk,cke->cqe', grad_scores, key_rows, preferred_element_type=...  36 us
    reshape x6, matrix products, group_step(): value_terms.reshape(in_group, slot_count, block_rows, head_width)  25.7 us
    dot_general x6, matrix products, group_step(): jnp.einsum('cqk,cke->cqe', attn_low, value_rows, preferred_element_type=j...  21 us
  transfers between devices with their start and end apart: 7, of which 3 were waited for; matrix products, arithmetic and copies ran while one was open for 59% of the time, Pallas kernels for 0%

commit v1 on v0

--- a/solution.py
+++ b/solution.py
@@ -1,3 +1,4 @@
+import functools
 import math
 import jax
 import jax.numpy as jnp
@@ -6,6 +7,30 @@
 
 HEADS = 16
 HD = 64
+
+
+def shifts_all_do(block_here, bus_axis):
+    q_next = jax.lax.axis_index(bus_axis)
+    side_arr = jax.lax.axis_size(bus_axis)
+    z, top = (side_arr, q_next)
+    ready = block_here.shape[0] // z
+    y_new = list(block_here.shape)
+    y_new[0] = ready
+    inter = y_new[1]
+    y_new[1] = inter * z
+    small = jnp.zeros(y_new, block_here.dtype)
+    for m in range(z):
+        after = lax.dynamic_slice_in_dim(block_here, (top ^ m) * ready, ready, axis=0)
+        if m:
+            h_now = range(z)
+            last = map(lambda no: (no, no ^ m), h_now)
+            reached = list(last)
+            after = jax.lax.ppermute(after, bus_axis, reached)
+        small = lax.dynamic_update_slice_in_dim(small, after, (top ^ m) * inter, axis=1)
+    return small
+
+
+fill_surface_on = functools.partial(shifts_all_do, bus_axis="seq")
 
 
 def attend(query, key_in, value, grad_out, blocks, counts):
@@ -118,7 +143,7 @@
     output_nodes = output_all[inverse]
     output_back, grad_back = (
         lax.all_to_all(output_nodes, "seq", split_axis=0, concat_axis=1, tiled=True),
-        lax.all_to_all(grad_heads, "seq", split_axis=0, concat_axis=1, tiled=True),
+        fill_surface_on(grad_heads),
     )
     attended = output_back.reshape(1, local_rows, model_width)
     grad_local = grad_back.reshape(local_rows, 3 * model_width)

time: 633 us -> 607 us (0.959)
  the two profiles are of different devices: /device:TPU:8 before, /device:TPU:34 now
where the time goes in v1:
time: 607 us; the launch traced here: 602 us
  local copies, waits for them, and re-layouts  167 us (28%)
  matrix products  166 us (27%)
  other arithmetic  95.1 us (16%)
  starting transfers between devices  81.9 us (13%)
  waiting for transfers between devices  77.1 us (13%)
  between operations  14.8 us (2%)
    all_gather x1, waiting for transfers between devices, per_device(): weights_all = lax.all_gather(qkv_weight, 'dp', axis=0, tiled=True)  71.8 us
    ppermute x15, starting transfers between devices, shifts_all_do(): after = jax.lax.ppermute(after, bus_axis, reached)  58.3 us
    dynamic_update_slice x16, local copies, waits for them, and re-layouts, shifts_all_do(): lax.dynamic_update_slice_in_dim(small, after, (top ^ m) * inter, axis=1)  43.4 us
    scatter-add x6, other arithmetic, group_step(): grad_value.at[block_ids]  42 us
    scatter-add x6, other arithmetic, group_step(): grad_key.at[block_ids]  42 us
    reshape x6, matrix products, group_step(): key_terms.reshape(in_group, slot_count, block_rows, head_width)  41.5 us
    dot_general x6, matrix products, group_step(): jnp.einsum('cqk,cke->cqe', grad_scores, key_rows, preferred_element_type=...  35.5 us
    reshape x6, matrix products, group_step(): value_terms.reshape(in_group, slot_count, block_rows, head_width)  25.6 us
  transfers between devices with their start and end apart: 21, of which 2 were waited for; matrix products, arithmetic and copies ran while one was open for 69% of the time, Pallas kernels for 0%

profile of v1, /device:TPU:34, one launch (start us, length us, event | category | flops | bytes accessed | tf_op | source)
XLA Modules:
  0.0 602.5 jit_solution(15964244420693973315)
XLA Ops:
  9.9 7.5 %all-to-all-start.1 = ((bf16[192,16,64]{0,2,1:T(8,128)(2,1)}), bf16[192,16,64]{0,2,1:T(8,128)(2,1)S(1)}, u32[]{:S(2)}, u32[]{:S(2)}) async-start(bf16[192,16,64]{0,2,1:T(8,128)(2,1)} %bitcast.27), calls=%async_computation.1 | async-start | bytes 1048576 | tf_op jit(solution)/shard_map/all_to_all | solution.py:122
  19.6 71.8 %all-gather.4.cloned.1.call-done = bf16[1024,3072]{1,0:T(8,128)(2,1)} async-done(((bf16[32,3072]{1,0:T(8,128)(2,1)}), bf16[1024,3072]{1,0:T(8,128)(2,1)}) %all-gather.4.cloned.1.call-update) | async-done | bytes 6291472 | tf_op jit(solution)/shard_map/all_gather | solution.py:113
  101.4 7.4 %all-to-all-start = ((bf16[192,16,192]{2,0,1:T(8,128)(2,1)}), bf16[192,16,192]{2,0,1:T(8,128)(2,1)S(1)}, u32[]{:S(2)}, u32[]{:S(2)}) async-start(bf16[192,16,192]{2,0,1:T(8,128)(2,1)} %copy.121), calls=%async_computation | async-start | bytes 3145728 | tf_op jit(solution)/shard_map/all_to_all | solution.py:121
  108.9 12.0 %scatter_custom_fusion.2 = s32[3072]{0:T(1024)S(1)} fusion(s32[3072]{0:T(1024)S(1)} %bitcast.204, s32[3072]{0:T(1024)S(1)} %iota.7, s32[]{:T(128)} %constant.7.clone.1), kind=kCustom, calls=%fused_computation.87 | custom fusion | bytes 12292 | tf_op jit(solution)/shard_map/scatter | solution.py:128
  121.3 11.4 %gather_fusion.3 = bf16[3072,64]{1,0:T(8,128)(2,1)} fusion(bf16[3072,64]{1,0:T(8,128)(2,1)S(1)} %bitcast.185, s32[3072]{0:T(1024)S(1)} %broadcast_clamp_fusion), kind=kCustom, calls=%fused_computation.3 | custom fusion | bytes 798720 | tf_op jit(solution)/shard_map/gather | solution.py:131
  136.5 11.1 %gather_fusion.2 = bf16[3072,192]{1,0:T(8,128)(2,1)S(1)} fusion(bf16[3072,192]{1,0:T(8,128)(2,1)S(1)} %bitcast.176, s32[3072]{0:T(1024)S(1)} %broadcast_clamp_fusion), kind=kCustom, calls=%fused_computation.2 | custom fusion | bytes 2371584 | tf_op jit(solution)/shard_map/gather | solution.py:130
  149.8 284.6 %while.16 = (s32[]{:T(128)}, f32[1,48,64,64]{3,2,1,0:T(8,128)S(1)}, f32[1,48,64,64]{3,2,1,0:T(8,128)S(1)}, bf16[6,1,8,64,64]{4,3,2,1,0:T(8,128)(2,1)}, bf16[6,1,...) while((s32[]{:T(128)}, f32[1,48,64,64]{3,2,1,0:T(8,128)S(1)}, ...), condition=%wide.region_6.7_spmd, body=%wide.region_0.6_spmd.sunk | while | flops 209000192 | bytes 36499064 | solution.py:95
  172.8 7.0 %scatter_fusion.1 = f32[48,64,64]{2,1,0:T(8,128)S(1)} fusion(f32[48,64,64]{2,1,0:T(8,128)S(1)} %bitcast.179, s32[64]{0:T(128)S(1)} %reshape.356, f32[64,64,64]{2,1,0:T(8,128)} %bitcast.187), kind=kCustom, calls=%fused_computation.7.clone.1 | custom fusion | flops 262144 | bytes 3145984 | tf_op jit(solution)/shard_map/vmap()/while/body/eval_jaxpr/scatter-add | solution.py:89
  179.8 6.9 %fusion.110 = f32[8,512,64]{2,1,0:T(8,128)} fusion(f32[8,64,512]{2,1,0:T(8,128)} %fusion.106, bf16[6,1,8,64,64]{4,3,2,1,0:T(8,128)(2,1)} %get-tuple-element.282, s32[]{:T(128)} %get-tuple-element.263, f32[8,64,512]{2,1,0:T(8,128)} %get-tuple-element.249, f32[8,64]{1,0:T(8,128)S(1)} %get-tuple-element.250), kind=kOutput, calls=%fused_computation.26.clone.1 | convolution fusion | flops 35390464 | bytes 5382656 | tf_op jit(solution)/shard_map/vmap()/while/body/eval_jaxpr/reshape | solution.py:87
  186.8 7.0 %scatter_fusion = f32[48,64,64]{2,1,0:T(8,128)S(1)} fusion(f32[48,64,64]{2,1,0:T(8,128)S(1)} %bitcast.177, s32[64]{0:T(128)S(1)} %reshape.356, f32[64,64,64]{2,1,0:T(8,128)} %bitcast.186), kind=kCustom, calls=%fused_computation.6.clone.1 | custom fusion | flops 262144 | bytes 3145984 | tf_op jit(solution)/shard_map/vmap()/while/body/eval_jaxpr/scatter-add | solution.py:86
  220.3 7.0 %scatter_fusion.1 = f32[48,64,64]{2,1,0:T(8,128)S(1)} fusion(f32[48,64,64]{2,1,0:T(8,128)S(1)} %bitcast.179, s32[64]{0:T(128)S(1)} %reshape.356, f32[64,64,64]{2,1,0:T(8,128)} %bitcast.187), kind=kCustom, calls=%fused_computation.7.clone.1 | custom fusion | flops 262144 | bytes 3145984 | tf_op jit(solution)/shard_map/vmap()/while/body/eval_jaxpr/scatter-add | solution.py:89
  227.3 6.9 %fusion.110 = f32[8,512,64]{2,1,0:T(8,128)} fusion(f32[8,64,512]{2,1,0:T(8,128)} %fusion.106, bf16[6,1,8,64,64]{4,3,2,1,0:T(8,128)(2,1)} %get-tuple-element.282, s32[]{:T(128)} %get-tuple-element.263, f32[8,64,512]{2,1,0:T(8,128)} %get-tuple-element.249, f32[8,64]{1,0:T(8,128)S(1)} %get-tuple-element.250), kind=kOutput, calls=%fused_computation.26.clone.1 | convolution fusion | flops 35390464 | bytes 5382656 | tf_op jit(solution)/shard_map/vmap()/while/body/eval_jaxpr/reshape | solution.py:87
  234.2 7.0 %scatter_fusion = f32[48,64,64]{2,1,0:T(8,128)S(1)} fusion(f32[48,64,64]{2,1,0:T(8,128)S(1)} %bitcast.177, s32[64]{0:T(128)S(1)} %reshape.356, f32[64,64,64]{2,1,0:T(8,128)} %bitcast.186), kind=kCustom, calls=%fused_computation.6.clone.1 | custom fusion | flops 262144 | bytes 3145984 | tf_op jit(solution)/shard_map/vmap()/while/body/eval_jaxpr/scatter-add | solution.py:86
  267.7 7.0 %scatter_fusion.1 = f32[48,64,64]{2,1,0:T(8,128)S(1)} fusion(f32[48,64,64]{2,1,0:T(8,128)S(1)} %bitcast.179, s32[64]{0:T(128)S(1)} %reshape.356, f32[64,64,64]{2,1,0:T(8,128)} %bitcast.187), kind=kCustom, calls=%fused_computation.7.clone.1 | custom fusion | flops 262144 | bytes 3145984 | tf_op jit(solution)/shard_map/vmap()/while/body/eval_jaxpr/scatter-add | solution.py:89
  274.7 6.9 %fusion.110 = f32[8,512,64]{2,1,0:T(8,128)} fusion(f32[8,64,512]{2,1,0:T(8,128)} %fusion.106, bf16[6,1,8,64,64]{4,3,2,1,0:T(8,128)(2,1)} %get-tuple-element.282, s32[]{:T(128)} %get-tuple-element.263, f32[8,64,512]{2,1,0:T(8,128)} %get-tuple-element.249, f32[8,64]{1,0:T(8,128)S(1)} %get-tuple-element.250), kind=kOutput, calls=%fused_computation.26.clone.1 | convolution fusion | flops 35390464 | bytes 5382656 | tf_op jit(solution)/shard_map/vmap()/while/body/eval_jaxpr/reshape | solution.py:87
  281.6 7.0 %scatter_fusion = f32[48,64,64]{2,1,0:T(8,128)S(1)} fusion(f32[48,64,64]{2,1,0:T(8,128)S(1)} %bitcast.177, s32[64]{0:T(128)S(1)} %reshape.356, f32[64,64,64]{2,1,0:T(8,128)} %bitcast.186), kind=kCustom, calls=%fused_computation.6.clone.1 | custom fusion | flops 262144 | bytes 3145984 | tf_op jit(solution)/shard_map/vmap()/while/body/eval_jaxpr/scatter-add | solution.py:86
  315.1 7.0 %scatter_fusion.1 = f32[48,64,64]{2,1,0:T(8,128)S(1)} fusion(f32[48,64,64]{2,1,0:T(8,128)S(1)} %bitcast.179, s32[64]{0:T(128)S(1)} %reshape.356, f32[64,64,64]{2,1,0:T(8,128)} %bitcast.187), kind=kCustom, calls=%fused_computation.7.clone.1 | custom fusion | flops 262144 | bytes 3145984 | tf_op jit(solution)/shard_map/vmap()/while/body/eval_jaxpr/scatter-add | solution.py:89
  322.1 6.9 %fusion.110 = f32[8,512,64]{2,1,0:T(8,128)} fusion(f32[8,64,512]{2,1,0:T(8,128)} %fusion.106, bf16[6,1,8,64,64]{4,3,2,1,0:T(8,128)(2,1)} %get-tuple-element.282, s32[]{:T(128)} %get-tuple-element.263, f32[8,64,512]{2,1,0:T(8,128)} %get-tuple-element.249, f32[8,64]{1,0:T(8,128)S(1)} %get-tuple-element.250), kind=kOutput, calls=%fused_computation.26.clone.1 | convolution fusion | flops 35390464 | bytes 5382656 | tf_op jit(solution)/shard_map/vmap()/while/body/eval_jaxpr/reshape | solution.py:87
  329.1 7.0 %scatter_fusion = f32[48,64,64]{2,1,0:T(8,128)S(1)} fusion(f32[48,64,64]{2,1,0:T(8,128)S(1)} %bitcast.177, s32[64]{0:T(128)S(1)} %reshape.356, f32[64,64,64]{2,1,0:T(8,128)} %bitcast.186), kind=kCustom, calls=%fused_computation.6.clone.1 | custom fusion | flops 262144 | bytes 3145984 | tf_op jit(solution)/shard_map/vmap()/while/body/eval_jaxpr/scatter-add | solution.py:86
  362.5 7.0 %scatter_fusion.1 = f32[48,64,64]{2,1,0:T(8,128)S(1)} fusion(f32[48,64,64]{2,1,0:T(8,128)S(1)} %bitcast.179, s32[64]{0:T(128)S(1)} %reshape.356, f32[64,64,64]{2,1,0:T(8,128)} %bitcast.187), kind=kCustom, calls=%fused_computation.7.clone.1 | custom fusion | flops 262144 | bytes 3145984 | tf_op jit(solution)/shard_map/vmap()/while/body/eval_jaxpr/scatter-add | solution.py:89
  369.5 6.9 %fusion.110 = f32[8,512,64]{2,1,0:T(8,128)} fusion(f32[8,64,512]{2,1,0:T(8,128)} %fusion.106, bf16[6,1,8,64,64]{4,3,2,1,0:T(8,128)(2,1)} %get-tuple-element.282, s32[]{:T(128)} %get-tuple-element.263, f32[8,64,512]{2,1,0:T(8,128)} %get-tuple-element.249, f32[8,64]{1,0:T(8,128)S(1)} %get-tuple-element.250), kind=kOutput, calls=%fused_computation.26.clone.1 | convolution fusion | flops 35390464 | bytes 5382656 | tf_op jit(solution)/shard_map/vmap()/while/body/eval_jaxpr/reshape | solution.py:87
  376.5 7.0 %scatter_fusion = f32[48,64,64]{2,1,0:T(8,128)S(1)} fusion(f32[48,64,64]{2,1,0:T(8,128)S(1)} %bitcast.177, s32[64]{0:T(128)S(1)} %reshape.356, f32[64,64,64]{2,1,0:T(8,128)} %bitcast.186), kind=kCustom, calls=%fused_computation.6.clone.1 | custom fusion | flops 262144 | bytes 3145984 | tf_op jit(solution)/shard_map/vmap()/while/body/eval_jaxpr/scatter-add | solution.py:86
  399.8 5.9 fusion.113
  410.0 7.0 %scatter_fusion.1 = f32[48,64,64]{2,1,0:T(8,128)S(1)} fusion(f32[48,64,64]{2,1,0:T(8,128)S(1)} %bitcast.179, s32[64]{0:T(128)S(1)} %reshape.356, f32[64,64,64]{2,1,0:T(8,128)} %bitcast.187), kind=kCustom, calls=%fused_computation.7.clone.1 | custom fusion | flops 262144 | bytes 3145984 | tf_op jit(solution)/shard_map/vmap()/while/body/eval_jaxpr/scatter-add | solution.py:89
  417.0 6.9 %fusion.110 = f32[8,512,64]{2,1,0:T(8,128)} fusion(f32[8,64,512]{2,1,0:T(8,128)} %fusion.106, bf16[6,1,8,64,64]{4,3,2,1,0:T(8,128)(2,1)} %get-tuple-element.282, s32[]{:T(128)} %get-tuple-element.263, f32[8,64,512]{2,1,0:T(8,128)} %get-tuple-element.249, f32[8,64]{1,0:T(8,128)S(1)} %get-tuple-element.250), kind=kOutput, calls=%fused_computation.26.clone.1 | convolution fusion | flops 35390464 | bytes 5382656 | tf_op jit(solution)/shard_map/vmap()/while/body/eval_jaxpr/reshape | solution.py:87
  423.9 7.0 %scatter_fusion = f32[48,64,64]{2,1,0:T(8,128)S(1)} fusion(f32[48,64,64]{2,1,0:T(8,128)S(1)} %bitcast.177, s32[64]{0:T(128)S(1)} %reshape.356, f32[64,64,64]{2,1,0:T(8,128)} %bitcast.186), kind=kCustom, calls=%fused_computation.6.clone.1 | custom fusion | flops 262144 | bytes 3145984 | tf_op jit(solution)/shard_map/vmap()/while/body/eval_jaxpr/scatter-add | solution.py:86
  436.5 11.1 %gather_fusion.5 = bf16[3072,192]{1,0:T(8,128)(2,1)S(1)} fusion(bf16[3072,192]{1,0:T(8,128)(2,1)S(1)} %maximum_bitcast_fusion, s32[3072]{0:T(1024)S(1)} %fusion.52), kind=kCustom, calls=%fused_computation.5 | custom fusion | bytes 2371584 | tf_op jit(solution)/shard_map/gather | solution.py:142
  466.5 6.6 %collective-permute-start.4 = (bf16[192,1,192]{2,0,1:T(8,128)(2,1)S(1)}, bf16[192,1,192]{2,0,1:T(8,128)(2,1)S(1)}, u32[]{:S(2)}, u32[]{:S(2)}) collective-permute-start(bf16[192,1,192]{2,0,1:T(8,128)(2,1)S(1)} %get-tuple-element.171), channel_id=1, source_target_pairs={{0,5},{1,4},{2,7},{3,6},{4,1},{5,0},{6,3},{7,2},{8,13},{9,12},{10,... | collective-permute-start | bytes 221192 | tf_op jit(solution)/shard_map/ppermute | solution.py:28
  481.9 7.4 %collective-permute-start.8 = (bf16[192,1,192]{2,0,1:T(8,128)(2,1)S(1)}, bf16[192,1,192]{2,0,1:T(8,128)(2,1)S(1)}, u32[]{:S(2)}, u32[]{:S(2)}) collective-permute-start(bf16[192,1,192]{2,0,1:T(8,128)(2,1)S(1)} %get-tuple-element.167), channel_id=1, source_target_pairs={{0,9},{1,8},{2,11},{3,10},{4,13},{5,12},{6,15},{7,14},{8,1},{9,0},... | collective-permute-start | bytes 221192 | tf_op jit(solution)/shard_map/ppermute | solution.py:28
  498.7 8.1 %collective-permute-start.12 = (bf16[192,1,192]{2,0,1:T(8,128)(2,1)S(1)}, bf16[192,1,192]{2,0,1:T(8,128)(2,1)S(1)}, u32[]{:S(2)}, u32[]{:S(2)}) collective-permute-start(bf16[192,1,192]{2,0,1:T(8,128)(2,1)S(1)} %get-tuple-element.163), channel_id=1, source_target_pairs={{0,13},{1,12},{2,15},{3,14},{4,9},{5,8},{6,11},{7,10},{8,5},{9,4},... | collective-permute-start | bytes 221192 | tf_op jit(solution)/shard_map/ppermute | solution.py:28
  513.2 9.2 %gather_fusion.4 = bf16[3072,64]{1,0:T(8,128)(2,1)S(1)} fusion(bf16[3072,64]{1,0:T(8,128)(2,1)S(1)} %bitcast.188, s32[3072]{0:T(1024)S(1)} %fusion.52), kind=kCustom, calls=%fused_computation.4 | custom fusion | bytes 798720 | tf_op jit(solution)/shard_map/gather | solution.py:143
  525.6 8.6 %all-to-all-start.2 = ((bf16[16,2,6144]{2,1,0:T(2,128)(2,1)}), bf16[16,2,6144]{2,1,0:T(2,128)(2,1)S(1)}, u32[]{:S(2)}, u32[]{:S(2)}) async-start(bf16[16,2,6144]{2,1,0:T(2,128)(2,1)} %reshape.337), calls=%async_computation.2 | async-start | bytes 786432 | tf_op jit(solution)/shard_map/all_to_all | solution.py:145
  (230 shorter events, 283.9 us)
Async XLA Ops:
  7.2 84.3 %copy-start.3 = (bf16[1,192,1024]{2,1,0:T(8,128)(2,1)S(1)}, bf16[1,192,1024]{2,1,0:T(8,128)(2,1)}, u32[]{:S(2)}) copy-start(bf16[1,192,1024]{2,1,0:T(8,128)(2,1)} %param.8) | copy-start | bytes 1179652
  7.2 11.1 %copy-start.10 = (s32[1,48,8]{1,2,0:T(8,128)S(1)}, s32[1,48,8]{1,2,0:T(8,128)}, u32[]{:S(2)}) copy-start(s32[1,48,8]{1,2,0:T(8,128)} %param.12) | copy-start | bytes 4612
  7.2 11.7 %copy-start.11 = (s32[1,48]{1,0:T(1,128)S(1)}, s32[1,48]{1,0:T(1,128)}, u32[]{:S(2)}) copy-start(s32[1,48]{1,0:T(1,128)} %param.13) | copy-start | bytes 580
  7.2 84.3 %all-gather.4.cloned.1.call-start = ((), (), s32[]{:S(2)}) async-start(), calls=%async_computation.4 | async-start | bytes 6488064 | tf_op jit(solution)/shard_map/all_gather | solution.py:113
  9.9 91.5 %all-to-all-start.1 = ((bf16[192,16,64]{0,2,1:T(8,128)(2,1)}), bf16[192,16,64]{0,2,1:T(8,128)(2,1)S(1)}, u32[]{:S(2)}, u32[]{:S(2)}) async-start(bf16[192,16,64]{0,2,1:T(8,128)(2,1)} %bitcast.27), calls=%async_computation.1 | async-start | bytes 1048576 | tf_op jit(solution)/shard_map/all_to_all | solution.py:122
  17.4 430.2 %all-gather.6.cloned.1.call-start = ((), (), s32[]{:S(2)}) async-start(), calls=%async_computation.5 | async-start | bytes 6684672 | tf_op jit(solution)/shard_map/all_gather | solution.py:114
  101.4 7.5 %copy-start.9 = (s32[1,3072]{1,0:T(1,128)S(1)}, s32[1,3072]{1,0:T(1,128)}, u32[]{:S(2)}) copy-start(s32[1,3072]{1,0:T(1,128)} %param.11) | copy-start | bytes 36868
  101.4 35.1 %all-to-all-start = ((bf16[192,16,192]{2,0,1:T(8,128)(2,1)}), bf16[192,16,192]{2,0,1:T(8,128)(2,1)S(1)}, u32[]{:S(2)}, u32[]{:S(2)}) async-start(bf16[192,16,192]{2,0,1:T(8,128)(2,1)} %copy.121), calls=%async_computation | async-start | bytes 3145728 | tf_op jit(solution)/shard_map/all_to_all | solution.py:121
  108.8 485.6 %reduce-scatter.4.cloned.1.call-start = ((), (), s32[]{:S(2)}) async-start(), calls=%async_computation.6 | async-start | bytes 540672
  249.7 1.0 copy-start
  434.6 1.1 copy-start.2
  452.8 60.3 %copy-start.1 = (bf16[6,1,8,64,64]{4,3,2,1,0:T(8,128)(2,1)S(1)}, bf16[6,1,8,64,64]{4,3,2,1,0:T(8,128)(2,1)}, u32[]{:S(2)}) copy-start(bf16[6,1,8,64,64]{4,3,2,1,0:T(8,128)(2,1)} %get-tuple-element.63) | copy-start | bytes 1179652
  453.7 19.4 %collective-permute-start = (bf16[192,1,192]{2,0,1:T(8,128)(2,1)S(1)}, bf16[192,1,192]{2,0,1:T(8,128)(2,1)S(1)}, u32[]{:S(2)}, u32[]{:S(2)}) collective-permute-start(bf16[192,1,192]{2,0,1:T(8,128)(2,1)S(1)} %get-tuple-element.175), channel_id=1, source_target_pairs={{0,1},{1,0},{2,3},{3,2},{4,5},{5,4},{6,7},{7,6},{8,9},{9,8},{10,11... | collective-permute-start | bytes 221192 | tf_op jit(solution)/shard_map/ppermute | solution.py:28
  459.2 15.8 %collective-permute-start.1 = (bf16[192,1,192]{2,0,1:T(8,128)(2,1)S(1)}, bf16[192,1,192]{2,0,1:T(8,128)(2,1)S(1)}, u32[]{:S(2)}, u32[]{:S(2)}) collective-permute-start(bf16[192,1,192]{2,0,1:T(8,128)(2,1)S(1)} %get-tuple-element.174), channel_id=1, source_target_pairs={{0,2},{1,3},{2,0},{3,1},{4,6},{5,7},{6,4},{7,5},{8,10},{9,11},{10,... | collective-permute-start | bytes 221192 | tf_op jit(solution)/shard_map/ppermute | solution.py:28
  461.2 16.9 %collective-permute-start.2 = (bf16[192,1,192]{2,0,1:T(8,128)(2,1)S(1)}, bf16[192,1,192]{2,0,1:T(8,128)(2,1)S(1)}, u32[]{:S(2)}, u32[]{:S(2)}) collective-permute-start(bf16[192,1,192]{2,0,1:T(8,128)(2,1)S(1)} %get-tuple-element.173), channel_id=1, source_target_pairs={{0,3},{1,2},{2,1},{3,0},{4,7},{5,6},{6,5},{7,4},{8,11},{9,10},{10,... | collective-permute-start | bytes 221192 | tf_op jit(solution)/shard_map/ppermute | solution.py:28
  464.5 17.3 %collective-permute-start.3 = (bf16[192,1,192]{2,0,1:T(8,128)(2,1)S(1)}, bf16[192,1,192]{2,0,1:T(8,128)(2,1)S(1)}, u32[]{:S(2)}, u32[]{:S(2)}) collective-permute-start(bf16[192,1,192]{2,0,1:T(8,128)(2,1)S(1)} %get-tuple-element.172), channel_id=1, source_target_pairs={{0,4},{1,5},{2,6},{3,7},{4,0},{5,1},{6,2},{7,3},{8,12},{9,13},{10,... | collective-permute-start | bytes 221192 | tf_op jit(solution)/shard_map/ppermute | solution.py:28
  466.5 22.9 %collective-permute-start.4 = (bf16[192,1,192]{2,0,1:T(8,128)(2,1)S(1)}, bf16[192,1,192]{2,0,1:T(8,128)(2,1)S(1)}, u32[]{:S(2)}, u32[]{:S(2)}) collective-permute-start(bf16[192,1,192]{2,0,1:T(8,128)(2,1)S(1)} %get-tuple-element.171), channel_id=1, source_target_pairs={{0,5},{1,4},{2,7},{3,6},{4,1},{5,0},{6,3},{7,2},{8,13},{9,12},{10,... | collective-permute-start | bytes 221192 | tf_op jit(solution)/shard_map/ppermute | solution.py:28
  473.1 36.3 %copy-start.4 = (bf16[192,1,192]{2,0,1:T(8,128)(2,1)}, bf16[192,1,192]{2,0,1:T(8,128)(2,1)S(1)}, u32[]{:S(2)}) copy-start(bf16[192,1,192]{2,0,1:T(8,128)(2,1)S(1)} %collective-permute-done) | copy-start | bytes 221188
  473.1 18.2 %collective-permute-start.5 = (bf16[192,1,192]{2,0,1:T(8,128)(2,1)S(1)}, bf16[192,1,192]{2,0,1:T(8,128)(2,1)S(1)}, u32[]{:S(2)}, u32[]{:S(2)}) collective-permute-start(bf16[192,1,192]{2,0,1:T(8,128)(2,1)S(1)} %get-tuple-element.170), channel_id=1, source_target_pairs={{0,6},{1,7},{2,4},{3,5},{4,2},{5,3},{6,0},{7,1},{8,14},{9,15},{10,... | collective-permute-start | bytes 221192 | tf_op jit(solution)/shard_map/ppermute | solution.py:28
  475.0 19.8 %collective-permute-start.6 = (bf16[192,1,192]{2,0,1:T(8,128)(2,1)S(1)}, bf16[192,1,192]{2,0,1:T(8,128)(2,1)S(1)}, u32[]{:S(2)}, u32[]{:S(2)}) collective-permute-start(bf16[192,1,192]{2,0,1:T(8,128)(2,1)S(1)} %get-tuple-element.169), channel_id=1, source_target_pairs={{0,7},{1,6},{2,5},{3,4},{4,3},{5,2},{6,1},{7,0},{8,15},{9,14},{10,... | collective-permute-start | bytes 221192 | tf_op jit(solution)/shard_map/ppermute | solution.py:28
  478.1 20.6 %collective-permute-start.7 = (bf16[192,1,192]{2,0,1:T(8,128)(2,1)S(1)}, bf16[192,1,192]{2,0,1:T(8,128)(2,1)S(1)}, u32[]{:S(2)}, u32[]{:S(2)}) collective-permute-start(bf16[192,1,192]{2,0,1:T(8,128)(2,1)S(1)} %get-tuple-element.168), channel_id=1, source_target_pairs={{0,8},{1,9},{2,10},{3,11},{4,12},{5,13},{6,14},{7,15},{8,0},{9,1},... | collective-permute-start | bytes 221192 | tf_op jit(solution)/shard_map/ppermute | solution.py:28
  481.9 24.9 %collective-permute-start.8 = (bf16[192,1,192]{2,0,1:T(8,128)(2,1)S(1)}, bf16[192,1,192]{2,0,1:T(8,128)(2,1)S(1)}, u32[]{:S(2)}, u32[]{:S(2)}) collective-permute-start(bf16[192,1,192]{2,0,1:T(8,128)(2,1)S(1)} %get-tuple-element.167), channel_id=1, source_target_pairs={{0,9},{1,8},{2,11},{3,10},{4,13},{5,12},{6,15},{7,14},{8,1},{9,0},... | collective-permute-start | bytes 221192 | tf_op jit(solution)/shard_map/ppermute | solution.py:28
  489.3 20.0 %collective-permute-start.9 = (bf16[192,1,192]{2,0,1:T(8,128)(2,1)S(1)}, bf16[192,1,192]{2,0,1:T(8,128)(2,1)S(1)}, u32[]{:S(2)}, u32[]{:S(2)}) collective-permute-start(bf16[192,1,192]{2,0,1:T(8,128)(2,1)S(1)} %get-tuple-element.166), channel_id=1, source_target_pairs={{0,10},{1,11},{2,8},{3,9},{4,14},{5,15},{6,12},{7,13},{8,2},{9,3},... | collective-permute-start | bytes 221192 | tf_op jit(solution)/shard_map/ppermute | solution.py:28
  491.3 75.4 %collective-permute-start.10 = (bf16[192,1,192]{2,0,1:T(8,128)(2,1)}, bf16[192,1,192]{2,0,1:T(8,128)(2,1)}, u32[]{:S(2)}, u32[]{:S(2)}) collective-permute-start(bf16[192,1,192]{2,0,1:T(8,128)(2,1)} %get-tuple-element.165), channel_id=1, source_target_pairs={{0,11},{1,10},{2,9},{3,8},{4,15},{5,14},{6,13},{7,12},{8,3},{9,2},... | collective-permute-start | bytes 221192 | tf_op jit(solution)/shard_map/ppermute | solution.py:28
  494.8 75.6 %collective-permute-start.11 = (bf16[192,1,192]{2,0,1:T(8,128)(2,1)}, bf16[192,1,192]{2,0,1:T(8,128)(2,1)}, u32[]{:S(2)}, u32[]{:S(2)}) collective-permute-start(bf16[192,1,192]{2,0,1:T(8,128)(2,1)} %get-tuple-element.164), channel_id=1, source_target_pairs={{0,12},{1,13},{2,14},{3,15},{4,8},{5,9},{6,10},{7,11},{8,4},{9,5},... | collective-permute-start | bytes 221192 | tf_op jit(solution)/shard_map/ppermute | solution.py:28
  498.7 75.5 %collective-permute-start.12 = (bf16[192,1,192]{2,0,1:T(8,128)(2,1)S(1)}, bf16[192,1,192]{2,0,1:T(8,128)(2,1)S(1)}, u32[]{:S(2)}, u32[]{:S(2)}) collective-permute-start(bf16[192,1,192]{2,0,1:T(8,128)(2,1)S(1)} %get-tuple-element.163), channel_id=1, source_target_pairs={{0,13},{1,12},{2,15},{3,14},{4,9},{5,8},{6,11},{7,10},{8,5},{9,4},... | collective-permute-start | bytes 221192 | tf_op jit(solution)/shard_map/ppermute | solution.py:28
  507.5 69.7 %collective-permute-start.13 = (bf16[192,1,192]{2,0,1:T(8,128)(2,1)S(1)}, bf16[192,1,192]{2,0,1:T(8,128)(2,1)S(1)}, u32[]{:S(2)}, u32[]{:S(2)}) collective-permute-start(bf16[192,1,192]{2,0,1:T(8,128)(2,1)S(1)} %get-tuple-element.162), channel_id=1, source_target_pairs={{0,14},{1,15},{2,12},{3,13},{4,10},{5,11},{6,8},{7,9},{8,6},{9,7},... | collective-permute-start | bytes 221192 | tf_op jit(solution)/shard_map/ppermute | solution.py:28
  509.4 3.8 copy-start.7
  509.4 70.6 %collective-permute-start.14 = (bf16[192,1,192]{2,0,1:T(8,128)(2,1)S(1)}, bf16[192,1,192]{2,0,1:T(8,128)(2,1)S(1)}, u32[]{:S(2)}, u32[]{:S(2)}) collective-permute-start(bf16[192,1,192]{2,0,1:T(8,128)(2,1)S(1)} %get-tuple-element.161), channel_id=1, source_target_pairs={{0,15},{1,14},{2,13},{3,12},{4,11},{5,10},{6,9},{7,8},{8,7},{9,6},... | collective-permute-start | bytes 221192 | tf_op jit(solution)/shard_map/ppermute | solution.py:28
  525.6 64.8 %all-to-all-start.2 = ((bf16[16,2,6144]{2,1,0:T(2,128)(2,1)}), bf16[16,2,6144]{2,1,0:T(2,128)(2,1)S(1)}, u32[]{:S(2)}, u32[]{:S(2)}) async-start(bf16[16,2,6144]{2,1,0:T(2,128)(2,1)} %reshape.337), calls=%async_computation.2 | async-start | bytes 786432 | tf_op jit(solution)/shard_map/all_to_all | solution.py:145
  546.7 14.3 %copy-start.6 = (bf16[192,1,192]{2,0,1:T(8,128)(2,1)S(1)}, bf16[192,1,192]{2,0,1:T(8,128)(2,1)}, u32[]{:S(2)}) copy-start(bf16[192,1,192]{2,0,1:T(8,128)(2,1)} %copy-done.5) | copy-start | bytes 221188
  549.6 14.3 %copy-start.8 = (bf16[192,1,192]{2,0,1:T(8,128)(2,1)S(1)}, bf16[192,1,192]{2,0,1:T(8,128)(2,1)}, u32[]{:S(2)}) copy-start(bf16[192,1,192]{2,0,1:T(8,128)(2,1)} %copy-done.7) | copy-start | bytes 221188
  (6 other events, 5.5 us)
Sparse Core Ops, SparseCore 0:
  10.2 81.2 all-gather.3
  94.5 83.6 all-gather.5
  453.0 100.2 reduce-scatter.3
